TPU v7x, 32 devices: a whole 2x2x4 slice. The times are simulated.
32 devices in a mesh: freq: 4 (over x, core), tm: 8 (over z, y).
Axes of the slice: x: 2, y: 2, z: 4, core: 2. Of those that a mesh axis runs over, the one named last changes fastest.
Arguments:
- visibilities: float32 [8, 8, 1024], P('freq', None, 'tm'), may hold values from -6 to 6
- coherencies: bfloat16 [8, 8, 8, 1024], P('freq', None, None, 'tm'), may hold values from -2.09375 to 2.09375
- pairs: int32 [2, 1024], P(None, 'tm'), may hold values from 0 to 511, as said below
- gains_start: float32 [8, 8, 8, 512], P('freq'), may hold values from -0.9 to 1.9
- duals_start: float32 [8, 8, 8, 512], P('freq'), may hold values from -12 to 12
- poly_start: float32 [4, 8, 8, 512], replicated, may hold values from -0.6 to 1.6
Outputs:
- gains: float32 [8, 8, 8, 512], P('freq')
- duals: float32 [8, 8, 8, 512], P('freq')
- polynomial: float32 [4, 8, 8, 512], replicated
Inputs may be any that keep to these rules, and one draw needn't show every extreme that they name: `pairs`: each row names two different stations.
All inputs are finite; a program needn't handle non-finite values.
Results may differ from a plain program's by a relative error of at most 0.0003.
Values sent between devices are 32-bit elements; how exact they have to be, the bound alone decides.
A program may use at most 64 MiB of HBM per device.

v0:
```python
from functools import partial
import jax
import jax.numpy as jnp
from jax import lax
from jax.sharding import PartitionSpec as P

ITERS = 2
RHO = 16.0
HIGHEST = lax.Precision.HIGHEST


def split(block):
    return ([block[i] for i in range(4)], [block[i + 4] for i in range(4)])


def join(matrix):
    return jnp.stack(matrix[0] + matrix[1])


def adjoint(matrix):
    real_part, imag_part = matrix
    return (
        [real_part[0], real_part[2], real_part[1], real_part[3]],
        [-imag_part[0], -imag_part[2], -imag_part[1], -imag_part[3]],
    )


def product(left, right):
    left_real, left_imag = left
    right_real, right_imag = right
    out_real = []
    out_imag = []
    for row in range(2):
        for column in range(2):
            first = 2 * row
            out_real.append(
                left_real[first] * right_real[column]
                - left_imag[first] * right_imag[column]
                + left_real[first + 1] * right_real[column + 2]
                - left_imag[first + 1] * right_imag[column + 2]
            )
            out_imag.append(
                left_real[first] * right_imag[column]
                + left_imag[first] * right_real[column]
                + left_real[first + 1] * right_imag[column + 2]
                + left_imag[first + 1] * right_real[column + 2]
            )
    return (out_real, out_imag)


def normal(matrix):
    real_part, imag_part = matrix
    top_left = real_part[0] ** 2 + imag_part[0] ** 2 + real_part[1] ** 2 + imag_part[1] ** 2
    bottom_right = real_part[2] ** 2 + imag_part[2] ** 2 + real_part[3] ** 2 + imag_part[3] ** 2
    cross_real = (
        real_part[0] * real_part[2]
        + imag_part[0] * imag_part[2]
        + real_part[1] * real_part[3]
        + imag_part[1] * imag_part[3]
    )
    cross_imag = (
        imag_part[0] * real_part[2]
        - real_part[0] * imag_part[2]
        + imag_part[1] * real_part[3]
        - real_part[1] * imag_part[3]
    )
    return jnp.stack([top_left, bottom_right, cross_real, cross_imag])


def data_sums(gains, coherencies, visibilities, pairs):
    jones_first = split(jnp.take(gains, pairs[0], axis=2))
    jones_second = split(jnp.take(gains, pairs[1], axis=2))
    skymodel = split(coherencies.astype(jnp.float32))
    left = product(jones_first, skymodel)
    right = product(skymodel, adjoint(jones_second))
    model = jnp.sum(join(product(left, adjoint(jones_second))), axis=1)
    residual = split((visibilities - model)[:, None, :])
    first_terms = jnp.concatenate([join(product(residual, adjoint(right))), normal(right)], axis=0)
    second_terms = jnp.concatenate(
        [join(product(adjoint(residual), left)), normal(adjoint(left))], axis=0
    )
    terms = jnp.concatenate([first_terms, second_terms], axis=2)
    stations = jnp.concatenate([pairs[0], pairs[1]])
    flat = terms.reshape(-1, terms.shape[2]).T
    summed = jax.ops.segment_sum(flat, stations, num_segments=gains.shape[2])
    return summed.T.reshape(12, gains.shape[1], gains.shape[2])


def update(gains, duals, prior, sums, damping):
    direction = split(sums[:8] - duals - RHO * (gains - prior))
    top_left, bottom_right, cross_real, cross_imag = (sums[8], sums[9], sums[10], sums[11])
    shift = damping * 0.5 * (top_left + bottom_right) + RHO
    upper = top_left + shift
    lower = bottom_right + shift
    determinant = upper * lower - cross_real * cross_real - cross_imag * cross_imag
    zeros = jnp.zeros_like(determinant)
    inverse = (
        [
            lower / determinant,
            -cross_real / determinant,
            -cross_real / determinant,
            upper / determinant,
        ],
        [zeros, -cross_imag / determinant, cross_imag / determinant, zeros],
    )
    return gains + join(product(direction, inverse))


def basis_weights(count):
    position = (2.0 * jnp.arange(count).astype(jnp.float32) + 1.0) / count - 1.0
    basis = jnp.stack(
        [
            jnp.ones_like(position),
            position,
            1.5 * position * position - 0.5,
            2.5 * position * position * position - 1.5 * position,
        ],
        axis=1,
    )
    gram = jnp.dot(basis.T, basis, precision=HIGHEST)
    factor = jnp.linalg.cholesky(gram)
    weights = jax.scipy.linalg.cho_solve((factor, True), basis.T)
    return (basis, weights)


def shards(visibilities, coherencies, pairs, gains_start, duals_start, poly_start):
    channels = gains_start.shape[0]
    offset = lax.axis_index("freq") * channels
    basis, weights = basis_weights(channels * lax.axis_size("freq"))
    local_basis = lax.dynamic_slice_in_dim(basis, offset, channels, 0)
    local_weights = lax.dynamic_slice_in_dim(weights, offset, channels, 1)
    channel_sums = jax.vmap(data_sums, in_axes=(0, 0, 0, None))
    gains, duals = (gains_start, duals_start)
    prior = jnp.einsum("fj,jcks->fcks", local_basis, poly_start, precision=HIGHEST)
    for inner in range(ITERS):
        local_terms = channel_sums(gains, coherencies, visibilities, pairs)
        sums = lax.psum(local_terms, "tm")
        gains = jax.vmap(partial(update, damping=12.0 * 0.5**inner))(gains, duals, prior, sums)
    mixed = gains + duals / RHO
    partial_fit = jnp.einsum("jf,fcks->jcks", local_weights, mixed, precision=HIGHEST)
    polynomial = lax.psum(partial_fit, "freq")
    prior = jnp.einsum("fj,jcks->fcks", local_basis, polynomial, precision=HIGHEST)
    duals = duals + RHO * (gains - prior)
    return (gains, duals, polynomial)


def solution(mesh):
    placed = (
        P("freq", None, "tm"),
        P("freq", None, None, "tm"),
        P(None, "tm"),
        P("freq", None, None, None),
        P("freq", None, None, None),
        P(),
    )
    return jax.shard_map(
        shards,
        mesh=mesh,
        in_specs=placed,
        out_specs=(P("freq", None, None, None), P("freq", None, None, None), P()),
        check_vma=False,
    )
```

profile of v0, /device:TPU:0, one launch (start us, length us, event | category | flops | bytes accessed | tf_op | source)
XLA Modules:
  0.0 250.6 jit_solution(10916335076422849878)
XLA Ops:
  7.2 0.8 compare_and_fusion.1
  8.0 3.5 %copy.795 = f32[2,8,8,512]{2,1,3,0:T(8,128)} copy(f32[2,8,8,512]{3,2,1,0:T(8,128)} %param.11) | data formatting | bytes 524288 | tf_op args[3]
  11.5 2.9 %gather_fusion.1 = f32[128,2,8,8]{3,2,1,0:T(8,128)S(1)} fusion(f32[2,8,8,512]{2,1,3,0:T(8,128)} %copy.795, s32[1024]{0:T(1024)S(1)} %pad_clamp_fusion), kind=kCustom, calls=%fused_computation.1.clone | custom fusion | bytes 131584 | tf_op jit(solution)/shard_map/vmap(jit(_take))/gather | solution.py:72
  14.4 0.4 copy.799
  14.8 2.9 %gather_fusion = f32[128,2,8,8]{3,2,1,0:T(8,128)S(1)} fusion(f32[2,8,8,512]{2,1,3,0:T(8,128)} %copy.795, s32[1024]{0:T(1024)S(1)} %pad_clamp_fusion.1), kind=kCustom, calls=%fused_computation.clone | custom fusion | bytes 131584 | tf_op jit(solution)/shard_map/vmap(jit(_take))/gather | solution.py:71
  17.7 0.4 copy.796
  18.4 0.2 copy.870
  18.6 0.2 copy.801
  20.3 0.1 copy.818
  20.5 0.1 broadcast.1350.clone
  20.6 8.3 %scatter_fusion = f32[2,512,96]{2,0,1:T(2,128)S(1)} fusion(f32[2,512,96]{2,0,1:T(2,128)S(1)} %broadcast.1350.clone, s32[256]{0:T(256)S(1)} %pad_add_fusion, f32[256,2,96]{2,1,0:T(2,128)S(1)} %copy.818), kind=kCustom, calls=%fused_computation.4 | custom fusion | flops 49152 | bytes 590848 | tf_op jit(solution)/shard_map/vmap()/scatter-add | solution.py:85
  29.0 0.2 copy.819
  29.2 0.8 copy.820
  30.2 0.2 fusion.63
  30.4 0.1 copy.853
  30.5 0.4 cholesky.16
  30.9 0.6 compare_reduce_fusion
  31.5 0.6 fusion.31
  32.2 0.3 custom-call.10
  32.5 1.2 fusion.2
  33.8 70.9 %all-reduce.4.cloned.1.call-done = f32[2,12,8,512]{3,2,0,1:T(8,128)} async-done(((f32[2,12,8,512]{3,2,0,1:T(8,128)}), f32[2,12,8,512]{3,2,0,1:T(8,128)}) %all-reduce.4.cloned.1.call-update) | async-done | bytes 393232 | tf_op jit(solution)/shard_map/psum | solution.py:137
  104.7 1.1 fusion.5
  105.8 0.8 constant_dynamic-update-slice_fusion.31
  106.6 0.8 constant_dynamic-update-slice_fusion.30
  107.7 2.6 %copy.826 = f32[2,8,8,512]{2,1,3,0:T(8,128)} copy(f32[2,8,8,512]{3,2,0,1:T(8,128)S(1)} %bitcast_add_fusion.1) | data formatting | bytes 524288 | tf_op jit(solution)/shard_map/vmap()/add | solution.py:106
  110.3 2.9 %gather_fusion.2 = f32[128,2,8,8]{3,2,1,0:T(8,128)S(1)} fusion(f32[2,8,8,512]{2,1,3,0:T(8,128)} %copy.826, s32[1024]{0:T(1024)S(1)} %pad_clamp_fusion.1), kind=kCustom, calls=%fused_computation.2.clone | custom fusion | bytes 131584 | tf_op jit(solution)/shard_map/vmap(jit(_take))/gather | solution.py:71
  113.2 3.8 %gather_fusion.3 = f32[128,2,8,8]{3,2,1,0:T(8,128)} fusion(f32[2,8,8,512]{2,1,3,0:T(8,128)} %copy.826, s32[1024]{0:T(1024)S(1)} %pad_clamp_fusion), kind=kCustom, calls=%fused_computation.3.clone | custom fusion | bytes 131584 | tf_op jit(solution)/shard_map/vmap(jit(_take))/gather | solution.py:72
  117.0 0.4 copy.827
  117.4 1.6 copy.829
  119.2 0.2 copy.871
  120.9 0.1 copy.848
  121.1 0.1 broadcast.1350
  121.2 8.3 %scatter_fusion.1 = f32[2,512,96]{2,0,1:T(2,128)S(1)} fusion(f32[2,512,96]{2,0,1:T(2,128)S(1)} %broadcast.1350, s32[256]{0:T(256)S(1)} %pad_add_fusion, f32[256,2,96]{2,1,0:T(2,128)S(1)} %copy.848), kind=kCustom, calls=%fused_computation.5 | custom fusion | flops 49152 | bytes 590848 | tf_op jit(solution)/shard_map/vmap()/scatter-add | solution.py:85
  129.5 0.2 copy.849
  129.7 0.8 copy.850
  130.5 0.2 all-reduce.8.cloned.1.call-start
  130.8 0.2 fusion.32
  131.0 0.2 fusion.34
  131.2 70.4 %all-reduce.6.cloned.1.call-done = f32[2,12,8,512]{3,2,0,1:T(8,128)} async-done(((f32[2,12,8,512]{3,2,0,1:T(8,128)}), f32[2,12,8,512]{3,2,0,1:T(8,128)}) %all-reduce.6.cloned.1.call-update) | async-done | bytes 393232 | tf_op jit(solution)/shard_map/psum | solution.py:137
  201.5 1.1 fusion.4
  202.6 0.8 constant_dynamic-update-slice_fusion.63
  203.4 0.8 constant_dynamic-update-slice_fusion.62
  204.5 2.1 fusion.8
  206.6 0.7 copy.859
  207.3 31.9 %all-reduce.8.cloned.1.call-done = f32[4,8,8,512]{3,0,2,1:T(4,128)} async-done(((f32[4,8,8,512]{3,0,2,1:T(4,128)}), f32[4,8,8,512]{3,0,2,1:T(4,128)}) %all-reduce.8.cloned.1.call-update) | async-done | bytes 524304 | tf_op jit(solution)/shard_map/psum | solution.py:141
  239.2 2.0 fusion.38
  241.4 0.7 copy.860
  242.1 2.0 copy.861
  (131 shorter events, 3.7 us)
Async XLA Ops:
  7.2 25.3 %copy-start = (f32[4,8,8,512]{3,2,1,0:T(8,128)S(1)}, f32[4,8,8,512]{3,2,1,0:T(8,128)}, u32[]{:S(2)}) copy-start(f32[4,8,8,512]{3,2,1,0:T(8,128)} %param.13) | copy-start | bytes 1572868
  7.2 10.9 %copy-start.3 = (bf16[2,8,8,128]{3,2,1,0:T(8,128)(2,1)S(1)}, bf16[2,8,8,128]{3,2,1,0:T(8,128)(2,1)}, u32[]{:S(2)}) copy-start(bf16[2,8,8,128]{3,2,1,0:T(8,128)(2,1)} %param.9) | copy-start | bytes 98308
  7.2 97.5 %all-reduce.4.cloned.1.call-start = ((), (), s32[]{:S(2)}) async-start(), calls=%async_computation | async-start | bytes 786432 | tf_op jit(solution)/shard_map/psum | solution.py:137
  8.0 10.6 %copy-start.4 = (f32[2,8,128]{2,1,0:T(8,128)S(1)}, f32[2,8,128]{2,1,0:T(8,128)}, u32[]{:S(2)}) copy-start(f32[2,8,128]{2,1,0:T(8,128)} %param.8) | copy-start | bytes 24580
  11.5 7.5 %copy-start.5 = (s32[2,128]{1,0:T(2,128)S(1)}, s32[2,128]{1,0:T(2,128)}, u32[]{:S(2)}) copy-start(s32[2,128]{1,0:T(2,128)} %param.10) | copy-start | bytes 3076
  18.9 85.8 %copy-start.1 = (f32[2,8,8,512]{3,2,1,0:T(8,128)S(1)}, f32[2,8,8,512]{3,2,1,0:T(8,128)}, u32[]{:S(2)}) copy-start(f32[2,8,8,512]{3,2,1,0:T(8,128)} %param.12) | copy-start | bytes 786436
  18.9 85.8 %copy-start.2 = (f32[2,8,8,512]{3,2,1,0:T(8,128)S(1)}, f32[2,8,8,512]{3,2,1,0:T(8,128)}, u32[]{:S(2)}) copy-start(f32[2,8,8,512]{3,2,1,0:T(8,128)} %param.11) | copy-start | bytes 786436
  30.0 171.6 %all-reduce.6.cloned.1.call-start = ((), (), s32[]{:S(2)}) async-start(), calls=%async_computation.1 | async-start | bytes 786432 | tf_op jit(solution)/shard_map/psum | solution.py:137
  130.5 108.7 %all-reduce.8.cloned.1.call-start = ((), (), s32[]{:S(2)}) async-start(), calls=%async_computation.2 | async-start | bytes 1048576 | tf_op jit(solution)/shard_map/psum | solution.py:141
Sparse Core Ops, SparseCore 0:
  30.1 74.5 all-reduce.3
  130.7 70.8 all-reduce.5
  206.7 32.4 all-reduce.7
where the time goes:
time: 251 us
  waiting for transfers between devices  173 us (69%)
  local copies, waits for them, and re-layouts  30 us (12%)
  other arithmetic  26.6 us (11%)
  between operations  14.6 us (6%)
  matrix products  5.93 us (2%)
    psum x2, waiting for transfers between devices, shards(): sums = lax.psum(local_terms, 'tm')  141 us
    psum x1, waiting for transfers between devices, shards(): polynomial = lax.psum(partial_fit, 'freq')  31.9 us
    scatter-add x2, other arithmetic, data_sums(): summed = jax.ops.segment_sum(flat, stations, num_segments=gains.shape[2])  16.7 us
    gather x4, local copies, waits for them, and re-layouts, data_sums(): jones_second = split(jnp.take(gains, pairs[1], axis=2))  8.74 us
    unnamed x19, local copies, waits for them, and re-layouts  7.63 us
    gather x4, local copies, waits for them, and re-layouts, data_sums(): jones_first = split(jnp.take(gains, pairs[0], axis=2))  6.57 us
  transfers between devices with their start and end apart: 3, of which 3 were waited for; matrix products, arithmetic and copies ran while one was open for 2% of the time, Pallas kernels for 0%

commit v1 on v0

--- a/solution.py
+++ b/solution.py
@@ -134,7 +134,7 @@
     prior = jnp.einsum("fj,jcks->fcks", local_basis, poly_start, precision=HIGHEST)
     for inner in range(ITERS):
         local_terms = channel_sums(gains, coherencies, visibilities, pairs)
-        sums = lax.psum(local_terms, "tm")
+        sums = jnp.sum(lax.all_gather(local_terms, "tm"), axis=0)
         gains = jax.vmap(partial(update, damping=12.0 * 0.5**inner))(gains, duals, prior, sums)
     mixed = gains + duals / RHO
     partial_fit = jnp.einsum("jf,fcks->jcks", local_weights, mixed, precision=HIGHEST)

time: 251 us -> 226 us (0.900)
  waiting for transfers between devices: 173 us -> 149 us
    psum x2 -> x0, waiting for transfers between devices: 141 us -> none  [shards(): sums = lax.psum(local_terms, 'tm')]
    all_gather x0 -> x2, waiting for transfers between devices: none -> 117 us  [shards(): sums = jnp.sum(lax.all_gather(local_terms, 'tm'), axis=0)]
    reduce_sum x0 -> x2, other arithmetic: none -> 4.53 us  [shards(): sums = jnp.sum(lax.all_gather(local_terms, 'tm'), axis=0)]
    unnamed x54, other arithmetic: 4.19 us -> 0.99 us
where the time goes in v1:
time: 226 us
  waiting for transfers between devices  149 us (66%)
  local copies, waits for them, and re-layouts  29.9 us (13%)
  other arithmetic  26 us (12%)
  between operations  14.6 us (6%)
  matrix products  5.95 us (3%)
    all_gather x2, waiting for transfers between devices, shards(): sums = jnp.sum(lax.all_gather(local_terms, 'tm'), axis=0)  117 us
    psum x1, waiting for transfers between devices, shards(): polynomial = lax.psum(partial_fit, 'freq')  31.5 us
    scatter-add x2, other arithmetic, data_sums(): summed = jax.ops.segment_sum(flat, stations, num_segments=gains.shape[2])  16.7 us
    gather x4, local copies, waits for them, and re-layouts, data_sums(): jones_second = split(jnp.take(gains, pairs[1], axis=2))  8.74 us
    unnamed x19, local copies, waits for them, and re-layouts  7.63 us
    gather x4, local copies, waits for them, and re-layouts, data_sums(): jones_first = split(jnp.take(gains, pairs[0], axis=2))  6.57 us
    reduce_sum x2, other arithmetic, shards(): sums = jnp.sum(lax.all_gather(local_terms, 'tm'), axis=0)  4.53 us
  transfers between devices with their start and end apart: 3, of which 3 were waited for; matrix products, arithmetic and copies ran while one was open for 2% of the time, Pallas kernels for 0%

profile of v1, /device:TPU:0, one launch (start us, length us, event | category | flops | bytes accessed | tf_op | source)
XLA Modules:
  0.0 225.7 jit_solution(9591774348343620963)
XLA Ops:
  7.2 0.8 compare_and_fusion.1
  8.0 3.5 %copy.750 = f32[2,8,8,512]{2,1,3,0:T(8,128)} copy(f32[2,8,8,512]{3,2,1,0:T(8,128)} %param.11) | data formatting | bytes 524288 | tf_op args[3]
  11.5 2.9 %gather_fusion.1 = f32[128,2,8,8]{3,2,1,0:T(8,128)S(1)} fusion(f32[2,8,8,512]{2,1,3,0:T(8,128)} %copy.750, s32[1024]{0:T(1024)S(1)} %pad_clamp_fusion), kind=kCustom, calls=%fused_computation.1.clone | custom fusion | bytes 131584 | tf_op jit(solution)/shard_map/vmap(jit(_take))/gather | solution.py:72
  14.4 0.4 copy.754
  14.8 2.9 %gather_fusion = f32[128,2,8,8]{3,2,1,0:T(8,128)S(1)} fusion(f32[2,8,8,512]{2,1,3,0:T(8,128)} %copy.750, s32[1024]{0:T(1024)S(1)} %pad_clamp_fusion.1), kind=kCustom, calls=%fused_computation.clone | custom fusion | bytes 131584 | tf_op jit(solution)/shard_map/vmap(jit(_take))/gather | solution.py:71
  17.7 0.4 copy.751
  18.4 0.2 copy.833
  18.6 0.2 copy.756
  19.1 0.1 copy.759
  20.3 0.1 copy.773
  20.5 0.1 broadcast.1350.clone
  20.6 8.3 %scatter_fusion = f32[2,512,96]{2,0,1:T(2,128)S(1)} fusion(f32[2,512,96]{2,0,1:T(2,128)S(1)} %broadcast.1350.clone, s32[256]{0:T(256)S(1)} %pad_add_fusion, f32[256,2,96]{2,1,0:T(2,128)S(1)} %copy.773), kind=kCustom, calls=%fused_computation.4 | custom fusion | flops 49152 | bytes 590848 | tf_op jit(solution)/shard_map/vmap()/scatter-add | solution.py:85
  29.0 0.9 copy.774
  30.1 1.2 fusion.2
  31.4 61.5 %all-gather.3.cloned.1.call-done = f32[8,2,12,8,512]{4,3,2,1,0:T(8,128)} async-done(((f32[1,2,12,8,512]{4,3,2,1,0:T(8,128)}), f32[8,2,12,8,512]{4,3,2,1,0:T(8,128)}) %all-gather.3.cloned.1.call-update) | async-done | bytes 3145744 | tf_op jit(solution)/shard_map/all_gather | solution.py:137
  92.8 2.3 %reduce_sum.37 = f32[2,12,8,512]{3,2,1,0:T(8,128)S(1)} reduce(f32[8,2,12,8,512]{4,3,2,1,0:T(8,128)} %all-gather.3.cloned.1.call-done, f32[]{:T(128)} %constant.80.clone.1), dimensions={0}, to_apply=%region_2.4 | reduce | flops 688128 | bytes 3538948 | tf_op jit(solution)/shard_map/reduce_sum | solution.py:137
  95.1 0.1 fusion.5
  95.6 2.6 %copy.785 = f32[2,8,8,512]{2,1,3,0:T(8,128)} copy(f32[2,8,8,512]{3,2,0,1:T(8,128)S(1)} %bitcast_add_fusion.1) | data formatting | bytes 524288 | tf_op jit(solution)/shard_map/vmap()/add | solution.py:106
  98.2 2.9 %gather_fusion.2 = f32[128,2,8,8]{3,2,1,0:T(8,128)S(1)} fusion(f32[2,8,8,512]{2,1,3,0:T(8,128)} %copy.785, s32[1024]{0:T(1024)S(1)} %pad_clamp_fusion.1), kind=kCustom, calls=%fused_computation.2.clone | custom fusion | bytes 131584 | tf_op jit(solution)/shard_map/vmap(jit(_take))/gather | solution.py:71
  101.0 3.8 %gather_fusion.3 = f32[128,2,8,8]{3,2,1,0:T(8,128)} fusion(f32[2,8,8,512]{2,1,3,0:T(8,128)} %copy.785, s32[1024]{0:T(1024)S(1)} %pad_clamp_fusion), kind=kCustom, calls=%fused_computation.3.clone | custom fusion | bytes 131584 | tf_op jit(solution)/shard_map/vmap(jit(_take))/gather | solution.py:72
  104.9 0.4 copy.786
  105.3 1.6 copy.788
  107.1 0.2 copy.834
  107.7 0.1 copy.794
  108.1 0.1 copy.798
  108.8 0.1 copy.807
  108.9 0.1 broadcast.1350
  109.1 8.3 %scatter_fusion.1 = f32[2,512,96]{2,0,1:T(2,128)S(1)} fusion(f32[2,512,96]{2,0,1:T(2,128)S(1)} %broadcast.1350, s32[256]{0:T(256)S(1)} %pad_add_fusion, f32[256,2,96]{2,1,0:T(2,128)S(1)} %copy.807), kind=kCustom, calls=%fused_computation.5 | custom fusion | flops 49152 | bytes 590848 | tf_op jit(solution)/shard_map/vmap()/scatter-add | solution.py:85
  117.4 0.9 copy.808
  118.4 0.2 all-reduce.2.cloned.1.call-start
  118.6 0.2 fusion.63
  118.8 0.1 copy.816
  118.9 0.4 cholesky.16
  119.3 0.6 compare_reduce_fusion
  120.0 0.6 fusion.31
  120.6 0.3 custom-call.10
  121.0 0.2 fusion.32
  121.2 0.2 fusion.34
  121.4 55.9 %all-gather.5.cloned.1.call-done = f32[8,2,12,8,512]{4,3,2,1,0:T(8,128)} async-done(((f32[1,2,12,8,512]{4,3,2,1,0:T(8,128)}), f32[8,2,12,8,512]{4,3,2,1,0:T(8,128)}) %all-gather.5.cloned.1.call-update) | async-done | bytes 3145744 | tf_op jit(solution)/shard_map/all_gather | solution.py:137
  177.2 2.3 %reduce_sum.39 = f32[2,12,8,512]{3,2,1,0:T(8,128)S(1)} reduce(f32[8,2,12,8,512]{4,3,2,1,0:T(8,128)} %all-gather.5.cloned.1.call-done, f32[]{:T(128)} %constant.80.clone.1), dimensions={0}, to_apply=%region_5.7 | reduce | flops 688128 | bytes 3538948 | tf_op jit(solution)/shard_map/reduce_sum | solution.py:137
  179.5 0.1 fusion.4
  179.9 2.1 fusion.8
  182.1 0.7 copy.822
  182.8 31.5 %all-reduce.2.cloned.1.call-done = f32[4,8,8,512]{3,0,2,1:T(4,128)} async-done(((f32[4,8,8,512]{3,0,2,1:T(4,128)}), f32[4,8,8,512]{3,0,2,1:T(4,128)}) %all-reduce.2.cloned.1.call-update) | async-done | bytes 524304 | tf_op jit(solution)/shard_map/psum | solution.py:141
  214.3 2.0 fusion.38
  216.3 0.1 fusion.7
  216.4 0.7 copy.823
  217.2 2.0 copy.824
  (131 shorter events, 3.5 us)
Async XLA Ops:
  7.2 23.0 %copy-start = (f32[4,8,8,512]{3,2,1,0:T(8,128)S(1)}, f32[4,8,8,512]{3,2,1,0:T(8,128)}, u32[]{:S(2)}) copy-start(f32[4,8,8,512]{3,2,1,0:T(8,128)} %param.13) | copy-start | bytes 1572868
  7.2 10.9 %copy-start.3 = (bf16[2,8,8,128]{3,2,1,0:T(8,128)(2,1)S(1)}, bf16[2,8,8,128]{3,2,1,0:T(8,128)(2,1)}, u32[]{:S(2)}) copy-start(bf16[2,8,8,128]{3,2,1,0:T(8,128)(2,1)} %param.9) | copy-start | bytes 98308
  7.2 85.6 %all-gather.3.cloned.1.call-start = ((), (), s32[]{:S(2)}) async-start(), calls=%async_computation | async-start | bytes 3538944 | tf_op jit(solution)/shard_map/all_gather | solution.py:137
  8.0 10.6 %copy-start.4 = (f32[2,8,128]{2,1,0:T(8,128)S(1)}, f32[2,8,128]{2,1,0:T(8,128)}, u32[]{:S(2)}) copy-start(f32[2,8,128]{2,1,0:T(8,128)} %param.8) | copy-start | bytes 24580
  11.5 7.5 %copy-start.5 = (s32[2,128]{1,0:T(2,128)S(1)}, s32[2,128]{1,0:T(2,128)}, u32[]{:S(2)}) copy-start(s32[2,128]{1,0:T(2,128)} %param.10) | copy-start | bytes 3076
  19.9 75.2 %copy-start.1 = (f32[2,8,8,512]{3,2,1,0:T(8,128)S(1)}, f32[2,8,8,512]{3,2,1,0:T(8,128)}, u32[]{:S(2)}) copy-start(f32[2,8,8,512]{3,2,1,0:T(8,128)} %param.12) | copy-start | bytes 786436
  20.0 75.2 %copy-start.2 = (f32[2,8,8,512]{3,2,1,0:T(8,128)S(1)}, f32[2,8,8,512]{3,2,1,0:T(8,128)}, u32[]{:S(2)}) copy-start(f32[2,8,8,512]{3,2,1,0:T(8,128)} %param.11) | copy-start | bytes 786436
  29.9 147.3 %all-gather.5.cloned.1.call-start = ((), (), s32[]{:S(2)}) async-start(), calls=%async_computation.1 | async-start | bytes 3538944 | tf_op jit(solution)/shard_map/all_gather | solution.py:137
  118.4 95.9 %all-reduce.2.cloned.1.call-start = ((), (), s32[]{:S(2)}) async-start(), calls=%async_computation.2 | async-start | bytes 1048576 | tf_op jit(solution)/shard_map/psum | solution.py:141
Sparse Core Ops, SparseCore 0:
  30.1 62.7 all-gather.2
  118.5 58.6 all-gather.4
  182.2 32.0 all-reduce.1
